TPU v7x, 256 devices: a whole 4x4x8 slice. The times are simulated.
256 devices in a mesh: dp: 16 (over y, x), expert: 16 (over z, core).
Axes of the slice: x: 4, y: 4, z: 8, core: 2. Of those that a mesh axis runs over, the one named last changes fastest.
Arguments:
- tokens: bfloat16 [16384, 2048], P(('dp', 'expert')), may hold values from -6 to 6
- expert_ids: int32 [16384, 8], P(('dp', 'expert')), may hold values from 0 to 31, all different within a row; in each aligned block of 64 rows (0 to 63, 64 to 127, ...) at most 24 rows name the same one
- gate_fixed: int32 [16384, 8], P(('dp', 'expert')), may hold values from 1 to 65535
- scorer_id: int32 [1024], P(('dp', 'expert')), may hold values from 0 to 1
- direction_tags: bfloat16 [2, 2048], replicated, may hold values from -6 to 6
- w_gate: bfloat16 [32, 2048, 512], P('expert'), may hold values from -0.125 to 0.125
- w_up: bfloat16 [32, 2048, 512], P('expert'), may hold values from -0.125 to 0.125
- w_down: bfloat16 [32, 512, 2048], P('expert'), may hold values from -0.25 to 0.25
- score_head: float32 [2048], replicated, may hold values from -0.125 to 0.125
Outputs:
- mixed: bfloat16 [16384, 2048], P(('dp', 'expert'))
- pair_score: float32 [1024], P(('dp', 'expert'))
Inputs may be any that keep to these rules, and one draw needn't show every extreme that they name: `expert_ids`: each row names 8 different experts. Among the rows of one device no expert is named by more than 24 rows, and in some devices' rows an expert is named by exactly 24.
All inputs are finite; a program needn't handle non-finite values.
Results may differ from a plain program's by a relative error of at most 0.04.
Values may be sent and summed in bfloat16 or wider, within the bound.
A program may use at most 64 MiB of HBM per device.

v0:
```python
import jax
import jax.numpy as jnp
from jax import lax
from jax.sharding import PartitionSpec as P

SEQ_LEN = 16
MOST = 24


def from_partner(block, axis, bit):
    count = lax.axis_size(axis)
    route = []
    for low in range(count):
        high = low | 1 << bit
        if high != low and high < count:
            route += [(low, high), (high, low)]
    return lax.ppermute(block, axis, route)


def route_ranks(expert_ids, expert_total):
    flat_ids = expert_ids.reshape(-1)
    entry_count = flat_ids.shape[0]
    onehot = flat_ids[:, None] == jnp.arange(expert_total, dtype=jnp.int32)[None, :]
    positions = jnp.arange(entry_count, dtype=jnp.int32)
    earlier = (positions[:, None] > positions[None, :]).astype(jnp.bfloat16)
    counts = jnp.dot(earlier, onehot.astype(jnp.bfloat16), preferred_element_type=jnp.float32)
    rank_in = jnp.sum(jnp.where(onehot, counts, 0.0), axis=1).astype(jnp.int32)
    return rank_in.reshape(expert_ids.shape)


def body(
    tokens, expert_ids, gate_fixed, scorer_id, direction_tags, w_gate, w_up, w_down, score_head
):
    expert_count = lax.axis_size("expert")
    per_device = w_gate.shape[0]
    tok_rows, model_width = tokens.shape
    top_count = expert_ids.shape[1]
    which_tag = jnp.repeat(scorer_id, SEQ_LEN)[:, None]
    tag_rows = jnp.where(
        which_tag == 1, direction_tags[1][None, :], direction_tags[0][None, :]
    ).astype(jnp.float32)
    inputs = (tokens.astype(jnp.float32) + tag_rows).astype(jnp.bfloat16)
    fixed_val = gate_fixed.astype(jnp.float32)
    weight = fixed_val / jnp.sum(fixed_val, axis=1, keepdims=True)
    rank_in = route_ranks(expert_ids, per_device * expert_count)
    inputs_all, ids_all, weight_all, rank_all = (
        lax.all_gather(inputs, "expert", axis=0, tiled=True),
        lax.all_gather(expert_ids, "expert", axis=0, tiled=True),
        lax.all_gather(weight.astype(jnp.bfloat16), "expert", axis=0, tiled=True).astype(
            weight.dtype
        ),
        lax.all_gather(rank_in, "expert", axis=0, tiled=True),
    )
    my_index = lax.axis_index("expert")
    local_count = per_device * MOST
    ids_cube = ids_all.reshape(expert_count, tok_rows, top_count)
    rank_cube = rank_all.reshape(expert_count, tok_rows, top_count)
    weight_cube = weight_all.reshape(expert_count, tok_rows, top_count)
    local_slot = ids_cube - my_index * per_device
    is_mine = (local_slot >= 0) & (local_slot < per_device)
    local_key = jnp.where(is_mine, local_slot * MOST + rank_cube, -1)
    match = (
        local_key[:, None, :, :] == jnp.arange(local_count, dtype=jnp.int32)[None, :, None, None]
    )
    picker = jnp.any(match, axis=3).astype(jnp.bfloat16)
    slot_weight = jnp.sum(jnp.where(match, weight_cube[:, None, :, :], 0.0), axis=(2, 3)).reshape(
        expert_count, per_device, MOST
    )
    inputs_cube = inputs_all.reshape(expert_count, tok_rows, model_width)
    row_block = jnp.einsum(
        "sqt,std->sqd", picker, inputs_cube, preferred_element_type=jnp.float32
    ).astype(jnp.bfloat16)
    row_block = row_block.reshape(expert_count, per_device, MOST, model_width)
    gate_proj = jnp.einsum("nemd,edf->nemf", row_block, w_gate, preferred_element_type=jnp.float32)
    up_proj = jnp.einsum("nemd,edf->nemf", row_block, w_up, preferred_element_type=jnp.float32)
    hidden = (jax.nn.silu(gate_proj) * up_proj).astype(jnp.bfloat16)
    down_out = jnp.einsum("nemf,efd->nemd", hidden, w_down, preferred_element_type=jnp.float32)
    result = (slot_weight[..., None] * down_out).astype(jnp.bfloat16)
    partial_value = jnp.einsum(
        "sqt,sqd->std",
        picker,
        result.reshape(expert_count, local_count, model_width),
        preferred_element_type=jnp.float32,
    )
    partial_value = partial_value.reshape(expert_count * tok_rows, model_width)
    received = lax.all_to_all(
        partial_value.astype(jnp.bfloat16), "expert", split_axis=0, concat_axis=0, tiled=True
    ).astype(partial_value.dtype)
    summed = received.reshape(expert_count, tok_rows, model_width).sum(axis=0)
    mixed = summed.astype(jnp.bfloat16)
    token_score = jnp.dot(mixed.astype(jnp.float32), score_head, precision=lax.Precision.HIGHEST)
    seq_score = token_score.reshape(-1, SEQ_LEN).sum(axis=1)
    partner = from_partner(seq_score, "dp", lax.axis_size("dp").bit_length() - 2)
    pair_score = jnp.abs(seq_score - partner) + 0.5 * (seq_score + partner)
    return (mixed, pair_score)


def solution(mesh):
    return jax.shard_map(
        body,
        mesh=mesh,
        in_specs=(
            P(("dp", "expert"), None),
            P(("dp", "expert"), None),
            P(("dp", "expert"), None),
            P(("dp", "expert")),
            P(),
            P("expert", None, None),
            P("expert", None, None),
            P("expert", None, None),
            P(),
        ),
        out_specs=(P(("dp", "expert"), None), P(("dp", "expert"))),
        check_vma=False,
    )
```

profile of v0, /device:TPU:1, one launch (start us, length us, event | category | flops | bytes accessed | tf_op | source)
XLA Modules:
  0.0 203.0 jit_solution(7624634206513829561)
XLA Ops:
  7.2 0.7 broadcast_compare_fusion
  8.1 0.8 slice_reduce_fusion.1
  8.9 1.8 add_convert_fusion
  10.7 0.7 convert_reduce_fusion
  11.4 0.7 fusion.27
  12.1 21.4 %all-gather.2 = bf16[16,64,8]{1,2,0:T(8,128)(2,1)S(1)} all-gather(bf16[1,64,8]{1,2,0:T(8,128)(2,1)S(1)} %fusion.27), channel_id=1, replica_groups=mesh['dp'=16,'expert'=16] {'expert'}, dimensions={0}, use_global_device_ids=true | all-gather | bytes 17408 | tf_op jit(solution)/shard_map/all_gather | solution.py:49
  33.5 0.8 copy.28
  34.3 0.3 fusion.20
  34.8 14.6 %all-gather.1 = s32[16,64,8]{1,2,0:T(8,128)S(1)} all-gather(s32[1,64,8]{1,2,0:T(8,128)S(1)} %copy.29), channel_id=1, replica_groups=mesh['dp'=16,'expert'=16] {'expert'}, dimensions={0}, use_global_device_ids=true | all-gather | bytes 34816 | tf_op jit(solution)/shard_map/all_gather | solution.py:52
  49.4 16.2 %all-gather = s32[16,64,8]{1,2,0:T(8,128)S(1)} all-gather(s32[1,64,8]{1,2,0:T(8,128)} %bitcast.68), channel_id=1, replica_groups=mesh['dp'=16,'expert'=16] {'expert'}, dimensions={0}, use_global_device_ids=true | all-gather | bytes 34816 | tf_op jit(solution)/shard_map/all_gather | solution.py:48
  65.7 1.7 select_reduce_fusion
  67.4 1.2 fusion.9
  68.6 3.3 %convolution_convert_fusion.1 = bf16[16,48,2048]{2,1,0:T(8,128)(2,1)S(1)} fusion(pred[16,48,64]{2,1,0:T(8,128)(4,1)S(1)} %fusion.9, bf16[16,64,2048]{2,1,0:T(8,128)(2,1)} %bitcast.64), kind=kOutput, calls=%fused_computation.9 | convolution fusion | flops 202899456 | bytes 7389184 | tf_op jit(solution)/shard_map/sqt,std->sqd/dot_general | solution.py:70
  71.9 0.1 copy-done.2
  72.1 3.0 %fusion.5 = f32[2,16,24,512]{3,2,1,0:T(8,128)} fusion(bf16[2,2048,512]{2,1,0:T(8,128)(2,1)S(1)} %copy-done.2, bf16[16,2,24,2048]{3,2,1,0:T(8,128)(2,1)S(1)} %bitcast.65), kind=kOutput, calls=%fused_computation.6 | convolution fusion | flops 1610612736 | bytes 8912896 | tf_op jit(solution)/shard_map/nemd,edf->nemf/dot_general | solution.py:74
  75.0 9.2 %fusion = bf16[16,2,24,2048]{3,2,0,1:T(8,128)(2,1)} fusion(bf16[2,512,2048]{2,1,0:T(8,128)(2,1)} %param.16, f32[16,2,24]{2,0,1:T(8,128)S(1)} %copy.30, f32[2,16,24,512]{3,2,1,0:T(8,128)} %fusion.5, bf16[2,2048,512]{2,1,0:T(8,128)(2,1)} %param.15, bf16[16,2,24,2048]{3,2,1,0:T(8,128)(2,1)S(1)} %bitcast.66), kind=kOutput, calls=%fused_computation.1 | convolution fusion | flops 3226730496 | bytes 16256000 | tf_op jit(solution)/shard_map/nemf,efd->nemd/dot_general | solution.py:77
  84.2 2.3 %copy.33 = bf16[16,2,24,2048]{3,2,1,0:T(8,128)(2,1)S(1)} copy(bf16[16,2,24,2048]{3,2,0,1:T(8,128)(2,1)} %fusion) | data formatting | bytes 6291456 | tf_op jit(solution)/shard_map/convert_element_type | solution.py:78
  86.5 1.3 convolution_convert_fusion
  87.8 99.7 %all_to_all.6 = bf16[16,64,2048]{2,1,0:T(8,128)(2,1)} all-to-all(bf16[16,64,2048]{2,1,0:T(8,128)(2,1)S(1)} %convolution_convert_fusion), channel_id=1, replica_groups=mesh['dp'=16,'expert'=16] {'expert'}, dimensions={0} | all-to-all | bytes 8388608 | tf_op jit(solution)/shard_map/all_to_all | solution.py:86
  187.5 3.0 %reduce_sum.51 = bf16[64,2048]{1,0:T(8,128)(2,1)S(1)} reduce(bf16[16,64,2048]{2,1,0:T(8,128)(2,1)} %all_to_all.6, bf16[]{:T(256)} %constant.24.clone.1), dimensions={0}, to_apply=%region_4.5 | reduce | flops 1966080 | bytes 4456450 | tf_op jit(solution)/shard_map/reduce_sum | solution.py:89
  190.5 1.0 fusion.29
  191.6 3.0 %collective-permute-start = (f32[4]{0:T(128)S(1)}, f32[4]{0:T(128)S(1)}, u32[]{:S(2)}, u32[]{:S(2)}) collective-permute-start(f32[4]{0:T(128)S(1)} %reduce_sum.52), channel_id=1, source_target_pairs={{0,128},{128,0},{16,144},{144,16},{32,160},{160,32},{48,176},{176,... | collective-permute-start | bytes 56 | tf_op jit(solution)/shard_map/ppermute | solution.py:17
  194.6 1.0 collective-permute-done
  195.6 0.5 multiply_add_fusion
  (19 shorter events, 0.7 us)
Async XLA Ops:
  7.2 183.3 %copy-start = (f32[2048]{0:T(1024)S(1)}, f32[2048]{0:T(1024)}, u32[]{:S(2)}) copy-start(f32[2048]{0:T(1024)} %param.17) | copy-start | bytes 24580
  7.2 61.4 %all-gather.5.cloned.1.call-start = ((), (), s32[]{:S(2)}) async-start(), calls=%async_computation.1 | async-start | bytes 4456448 | tf_op jit(solution)/shard_map/all_gather | solution.py:47
  68.6 3.5 %copy-start.2 = (bf16[2,2048,512]{2,1,0:T(8,128)(2,1)S(1)}, bf16[2,2048,512]{2,1,0:T(8,128)(2,1)}, u32[]{:S(2)}) copy-start(bf16[2,2048,512]{2,1,0:T(8,128)(2,1)} %param.14) | copy-start | bytes 12582916
  190.5 5.7 %copy-start.1 = (bf16[64,2048]{1,0:T(8,128)(2,1)}, bf16[64,2048]{1,0:T(8,128)(2,1)S(1)}, u32[]{:S(2)}) copy-start(bf16[64,2048]{1,0:T(8,128)(2,1)S(1)} %reduce_sum.51) | copy-start | bytes 786436
  191.6 4.0 %collective-permute-start = (f32[4]{0:T(128)S(1)}, f32[4]{0:T(128)S(1)}, u32[]{:S(2)}, u32[]{:S(2)}) collective-permute-start(f32[4]{0:T(128)S(1)} %reduce_sum.52), channel_id=1, source_target_pairs={{0,128},{128,0},{16,144},{144,16},{32,160},{160,32},{48,176},{176,... | collective-permute-start | bytes 56 | tf_op jit(solution)/shard_map/ppermute | solution.py:17
Sparse Core Ops, SparseCore 0:
  10.8 46.5 all-gather.4
where the time goes:
time: 203 us
  blocking collectives  152 us (75%)
  matrix products  18 us (9%)
  between operations  14.2 us (7%)
  other arithmetic  10.3 us (5%)
  local copies, waits for them, and re-layouts  4.53 us (2%)
  starting transfers between devices  3.04 us (1%)
    all_to_all x1, blocking collectives, body(): lax.all_to_all(partial_value.astype(jnp.bfloat16), 'expert', split_axis=0...  99.7 us
    all_gather x1, blocking collectives, body(): lax.all_gather(weight.astype(jnp.bfloat16), 'expert', axis=0, tiled=True)  21.4 us
    all_gather x1, blocking collectives, body(): lax.all_gather(expert_ids, 'expert', axis=0, tiled=True)  16.2 us
    all_gather x1, blocking collectives, body(): lax.all_gather(rank_in, 'expert', axis=0, tiled=True)  14.6 us
    dot_general x1, matrix products, body(): jnp.einsum('nemf,efd->nemd', hidden, w_down, preferred_element_type=jnp.f...  9.16 us
  transfers between devices with their start and end apart: 2, of which 1 were waited for; matrix products, arithmetic and copies ran while one was open for 3% of the time, Pallas kernels for 0%

commit v1 on v0

--- a/solution.py
+++ b/solution.py
@@ -5,6 +5,12 @@
 
 SEQ_LEN = 16
 MOST = 24
+
+
+def replace_gates(raw, axis_k):
+    raw = jnp.moveaxis(raw, 0, axis_k)
+    z2 = raw.shape
+    return raw.reshape(*z2[:axis_k], z2[axis_k] * z2[axis_k + 1], *z2[axis_k + 2 :])
 
 
 def from_partner(block, axis, bit):
@@ -31,6 +37,36 @@
 def body(
     tokens, expert_ids, gate_fixed, scorer_id, direction_tags, w_gate, w_up, w_down, score_head
 ):
+
+    def switch_loops(frame, axis_id, k_dim):
+        nd = jax.lax.axis_size(axis_id)
+        pile = []
+        w = 0
+        while w < nd:
+            pile.append((w, (w + 1) % nd))
+            w += 1
+        log = []
+        for k, tick in pile:
+            log.append((tick, k))
+        extra, moved = ([], [])
+        d = 0
+        while d < nd - 1:
+            if d % 2 == 0:
+                extra.append(
+                    jax.lax.ppermute(extra[-1] if extra else frame, axis_name=axis_id, perm=pile)
+                )
+            else:
+                moved.append(
+                    jax.lax.ppermute(moved[-1] if moved else frame, axis_name=axis_id, perm=log)
+                )
+            d = d + 1
+        spare = jnp.stack([*extra[::-1], frame, *moved], axis=0)
+        v1 = jax.lax.axis_index(axis_id)
+        ready = len(extra)
+        outer = v1 - ready
+        spare = spare[(jnp.arange(nd) - outer) % nd]
+        return replace_gates(spare, k_dim)
+
     expert_count = lax.axis_size("expert")
     per_device = w_gate.shape[0]
     tok_rows, model_width = tokens.shape
@@ -45,7 +81,7 @@
     rank_in = route_ranks(expert_ids, per_device * expert_count)
     inputs_all, ids_all, weight_all, rank_all = (
         lax.all_gather(inputs, "expert", axis=0, tiled=True),
-        lax.all_gather(expert_ids, "expert", axis=0, tiled=True),
+        switch_loops(expert_ids, "expert", 0),
         lax.all_gather(weight.astype(jnp.bfloat16), "expert", axis=0, tiled=True).astype(
             weight.dtype
         ),

time: 203 us -> 217 us (1.069)
  starting transfers between devices: 3.04 us -> 25 us
  blocking collectives: 152 us -> 135 us
  waiting for transfers between devices: 1.02 us -> 8.1 us
    ppermute x0 -> x15, starting transfers between devices: none -> 22.1 us  [the longest x7 15.2 us: switch_loops(): jax.lax.ppermute(moved[-1] if moved else frame, axis_name=axis_id, perm=log)]
    all_gather x1 -> x0, blocking collectives: 16.2 us -> none  [body(): lax.all_gather(expert_ids, 'expert', axis=0, tiled=True)]
    ppermute x0 -> x15, waiting for transfers between devices: none -> 6.91 us  [the longest x7 4.06 us: switch_loops(): jax.lax.ppermute(moved[-1] if moved else frame, axis_name=axis_id, perm=log)]
    all_gather x1, blocking collectives: 21.4 us -> 15.8 us  [body(): lax.all_gather(weight.astype(jnp.bfloat16), 'expert', axis=0, tiled=True)]
    all_gather x1, blocking collectives: 14.6 us -> 17.9 us  [body(): lax.all_gather(rank_in, 'expert', axis=0, tiled=True)]
  transfers between devices with their start and end apart: 2 -> 17, of which waited for: 1 -> 7; matrix products, arithmetic and copies ran while one was open for 3% -> 3% of each run, Pallas kernels for 0% -> 0%
where the time goes in v1:
time: 217 us; the launch traced here: 216 us
  blocking collectives  135 us (62%)
  starting transfers between devices  25 us (12%)
  matrix products  18 us (8%)
  between operations  14.3 us (7%)
  other arithmetic  10.3 us (5%)
  waiting for transfers between devices  8.1 us (4%)
  local copies, waits for them, and re-layouts  5.82 us (3%)
    all_to_all x1, blocking collectives, body(): lax.all_to_all(partial_value.astype(jnp.bfloat16), 'expert', split_axis=0...  101 us
    all_gather x1, blocking collectives, body(): lax.all_gather(rank_in, 'expert', axis=0, tiled=True)  17.9 us
    all_gather x1, blocking collectives, body(): lax.all_gather(weight.astype(jnp.bfloat16), 'expert', axis=0, tiled=True)  15.8 us
    ppermute x7, starting transfers between devices, switch_loops(): jax.lax.ppermute(moved[-1] if moved else frame, axis_name=axis_id, perm=log)  15.2 us
    dot_general x1, matrix products, body(): jnp.einsum('nemf,efd->nemd', hidden, w_down, preferred_element_type=jnp.f...  9.16 us
    ppermute x8, starting transfers between devices, switch_loops(): jax.lax.ppermute(extra[-1] if extra else frame, axis_name=axis_id, perm=p...  6.95 us
  transfers between devices with their start and end apart: 17, of which 7 were waited for; matrix products, arithmetic and copies ran while one was open for 3% of the time, Pallas kernels for 0%

profile of v1, /device:TPU:1, one launch (start us, length us, event | category | flops | bytes accessed | tf_op | source)
XLA Modules:
  0.0 216.2 jit_solution(3198029366911812746)
XLA Ops:
  8.9 1.8 add_convert_fusion
  10.7 3.0 %collective-permute-start = (s32[64,8]{0,1:T(8,128)}, s32[64,8]{0,1:T(8,128)S(1)}, u32[]{:S(2)}, u32[]{:S(2)}) collective-permute-start(s32[64,8]{0,1:T(8,128)} %param.10), channel_id=1, source_target_pairs={{0,1},{1,2},{2,3},{3,4},{4,5},{5,6},{6,7},{7,8},{8,9},{9,10},{10,1... | collective-permute-start | bytes 6152 | tf_op jit(solution)/shard_map/ppermute | solution.py:56
  14.8 2.2 collective-permute-start.1
  17.7 2.0 collective-permute-done.1
  21.6 3.3 %collective-permute-start.9 = (s32[64,8]{0,1:T(8,128)S(1)}, s32[64,8]{0,1:T(8,128)S(1)}, u32[]{:S(2)}, u32[]{:S(2)}) collective-permute-start(s32[64,8]{0,1:T(8,128)S(1)} %collective-permute-done.8), channel_id=1, source_target_pairs={{1,0},{2,1},{3,2},{4,3},{5,4},{6,5},{7,6},{8,7},{9,8},{10,9},{11,1... | collective-permute-start | bytes 6152 | tf_op jit(solution)/shard_map/ppermute | solution.py:60
  25.7 3.5 %collective-permute-start.10 = (s32[64,8]{0,1:T(8,128)S(1)}, s32[64,8]{0,1:T(8,128)S(1)}, u32[]{:S(2)}, u32[]{:S(2)}) collective-permute-start(s32[64,8]{0,1:T(8,128)S(1)} %collective-permute-done.9), channel_id=1, source_target_pairs={{1,0},{2,1},{3,2},{4,3},{5,4},{6,5},{7,6},{8,7},{9,8},{10,9},{11,1... | collective-permute-start | bytes 6152 | tf_op jit(solution)/shard_map/ppermute | solution.py:60
  29.9 3.9 %collective-permute-start.11 = (s32[64,8]{0,1:T(8,128)S(1)}, s32[64,8]{0,1:T(8,128)S(1)}, u32[]{:S(2)}, u32[]{:S(2)}) collective-permute-start(s32[64,8]{0,1:T(8,128)S(1)} %collective-permute-done.10), channel_id=1, source_target_pairs={{1,0},{2,1},{3,2},{4,3},{5,4},{6,5},{7,6},{8,7},{9,8},{10,9},{11,1... | collective-permute-start | bytes 6152 | tf_op jit(solution)/shard_map/ppermute | solution.py:60
  34.6 3.8 %collective-permute-start.12 = (s32[64,8]{0,1:T(8,128)S(1)}, s32[64,8]{0,1:T(8,128)S(1)}, u32[]{:S(2)}, u32[]{:S(2)}) collective-permute-start(s32[64,8]{0,1:T(8,128)S(1)} %collective-permute-done.11), channel_id=1, source_target_pairs={{1,0},{2,1},{3,2},{4,3},{5,4},{6,5},{7,6},{8,7},{9,8},{10,9},{11,1... | collective-permute-start | bytes 6152 | tf_op jit(solution)/shard_map/ppermute | solution.py:60
  38.4 17.9 %all-gather = s32[16,64,8]{1,2,0:T(8,128)S(1)} all-gather(s32[1,64,8]{1,2,0:T(8,128)S(1)} %copy.36), channel_id=1, replica_groups=mesh['dp'=16,'expert'=16] {'expert'}, dimensions={0}, use_global_device_ids=true | all-gather | bytes 34816 | tf_op jit(solution)/shard_map/all_gather | solution.py:88
  56.7 1.4 collective-permute-start.7
  58.1 15.8 %all-gather.1 = bf16[16,64,8]{1,2,0:T(8,128)(2,1)S(1)} all-gather(bf16[1,64,8]{1,2,0:T(8,128)(2,1)S(1)} %fusion.27), channel_id=1, replica_groups=mesh['dp'=16,'expert'=16] {'expert'}, dimensions={0}, use_global_device_ids=true | all-gather | bytes 17408 | tf_op jit(solution)/shard_map/all_gather | solution.py:85
  74.9 2.1 collective-permute-done.14
  77.6 1.7 select_reduce_fusion
  79.3 1.2 fusion.9
  80.6 3.3 %convolution_convert_fusion.1 = bf16[16,48,2048]{2,1,0:T(8,128)(2,1)S(1)} fusion(pred[16,48,64]{2,1,0:T(8,128)(4,1)S(1)} %fusion.9, bf16[16,64,2048]{2,1,0:T(8,128)(2,1)} %bitcast.97), kind=kOutput, calls=%fused_computation.10 | convolution fusion | flops 202899456 | bytes 7389184 | tf_op jit(solution)/shard_map/sqt,std->sqd/dot_general | solution.py:106
  84.0 3.0 %fusion.5 = f32[2,16,24,512]{3,2,1,0:T(8,128)} fusion(bf16[2,2048,512]{2,1,0:T(8,128)(2,1)S(1)} %copy-done.2, bf16[16,2,24,2048]{3,2,1,0:T(8,128)(2,1)S(1)} %bitcast.98), kind=kOutput, calls=%fused_computation.7 | convolution fusion | flops 1610612736 | bytes 8912896 | tf_op jit(solution)/shard_map/nemd,edf->nemf/dot_general | solution.py:110
  86.9 9.2 %fusion = bf16[16,2,24,2048]{3,2,0,1:T(8,128)(2,1)} fusion(bf16[2,512,2048]{2,1,0:T(8,128)(2,1)} %param.16, f32[16,2,24]{2,0,1:T(8,128)S(1)} %copy.37, f32[2,16,24,512]{3,2,1,0:T(8,128)} %fusion.5, bf16[2,2048,512]{2,1,0:T(8,128)(2,1)} %param.15, bf16[16,2,24,2048]{3,2,1,0:T(8,128)(2,1)S(1)} %bitcast.99), kind=kOutput, calls=%fused_computation.2 | convolution fusion | flops 3226730496 | bytes 16256000 | tf_op jit(solution)/shard_map/nemf,efd->nemd/dot_general | solution.py:113
  96.1 2.3 %copy.40 = bf16[16,2,24,2048]{3,2,1,0:T(8,128)(2,1)S(1)} copy(bf16[16,2,24,2048]{3,2,0,1:T(8,128)(2,1)} %fusion) | data formatting | bytes 6291456 | tf_op jit(solution)/shard_map/convert_element_type | solution.py:114
  98.4 1.3 convolution_convert_fusion
  99.7 101.0 %all_to_all.6 = bf16[16,64,2048]{2,1,0:T(8,128)(2,1)} all-to-all(bf16[16,64,2048]{2,1,0:T(8,128)(2,1)S(1)} %convolution_convert_fusion), channel_id=1, replica_groups=mesh['dp'=16,'expert'=16] {'expert'}, dimensions={0} | all-to-all | bytes 8388608 | tf_op jit(solution)/shard_map/all_to_all | solution.py:122
  200.7 3.0 %reduce_sum.51 = bf16[64,2048]{1,0:T(8,128)(2,1)S(1)} reduce(bf16[16,64,2048]{2,1,0:T(8,128)(2,1)} %all_to_all.6, bf16[]{:T(256)} %constant.43.clone.1), dimensions={0}, to_apply=%region_4.5 | reduce | flops 1966080 | bytes 4456450 | tf_op jit(solution)/shard_map/reduce_sum | solution.py:125
  203.7 1.0 fusion.31
  204.8 2.8 %collective-permute-start.15 = (f32[4]{0:T(128)S(1)}, f32[4]{0:T(128)S(1)}, u32[]{:S(2)}, u32[]{:S(2)}) collective-permute-start(f32[4]{0:T(128)S(1)} %reduce_sum.52), channel_id=1, source_target_pairs={{0,128},{128,0},{16,144},{144,16},{32,160},{160,32},{48,176},{176,... | collective-permute-start | bytes 56 | tf_op jit(solution)/shard_map/ppermute | solution.py:23
  207.7 1.2 collective-permute-done.15
  (67 shorter events, 10.6 us)
Async XLA Ops:
  7.2 196.5 %copy-start = (f32[2048]{0:T(1024)S(1)}, f32[2048]{0:T(1024)}, u32[]{:S(2)}) copy-start(f32[2048]{0:T(1024)} %param.17) | copy-start | bytes 24580
  7.2 73.4 %all-gather.4.cloned.1.call-start = ((), (), s32[]{:S(2)}) async-start(), calls=%async_computation.1 | async-start | bytes 4456448 | tf_op jit(solution)/shard_map/all_gather | solution.py:83
  10.7 4.1 %collective-permute-start = (s32[64,8]{0,1:T(8,128)}, s32[64,8]{0,1:T(8,128)S(1)}, u32[]{:S(2)}, u32[]{:S(2)}) collective-permute-start(s32[64,8]{0,1:T(8,128)} %param.10), channel_id=1, source_target_pairs={{0,1},{1,2},{2,3},{3,4},{4,5},{5,6},{6,7},{7,8},{8,9},{9,10},{10,1... | collective-permute-start | bytes 6152 | tf_op jit(solution)/shard_map/ppermute | solution.py:56
  13.7 7.8 %collective-permute-start.8 = (s32[64,8]{0,1:T(8,128)}, s32[64,8]{0,1:T(8,128)S(1)}, u32[]{:S(2)}, u32[]{:S(2)}) collective-permute-start(s32[64,8]{0,1:T(8,128)} %param.10), channel_id=1, source_target_pairs={{1,0},{2,1},{3,2},{4,3},{5,4},{6,5},{7,6},{8,7},{9,8},{10,9},{11,1... | collective-permute-start | bytes 6152 | tf_op jit(solution)/shard_map/ppermute | solution.py:60
  14.8 4.8 %collective-permute-start.1 = (s32[64,8]{0,1:T(8,128)S(1)}, s32[64,8]{0,1:T(8,128)S(1)}, u32[]{:S(2)}, u32[]{:S(2)}) collective-permute-start(s32[64,8]{0,1:T(8,128)S(1)} %collective-permute-done), channel_id=1, source_target_pairs={{0,1},{1,2},{2,3},{3,4},{4,5},{5,6},{6,7},{7,8},{8,9},{9,10},{10,1... | collective-permute-start | bytes 6152 | tf_op jit(solution)/shard_map/ppermute | solution.py:56
  19.7 5.2 %collective-permute-start.2 = (s32[64,8]{0,1:T(8,128)S(1)}, s32[64,8]{0,1:T(8,128)S(1)}, u32[]{:S(2)}, u32[]{:S(2)}) collective-permute-start(s32[64,8]{0,1:T(8,128)S(1)} %collective-permute-done.1), channel_id=1, source_target_pairs={{0,1},{1,2},{2,3},{3,4},{4,5},{5,6},{6,7},{7,8},{8,9},{9,10},{10,1... | collective-permute-start | bytes 6152 | tf_op jit(solution)/shard_map/ppermute | solution.py:56
  21.6 4.1 %collective-permute-start.9 = (s32[64,8]{0,1:T(8,128)S(1)}, s32[64,8]{0,1:T(8,128)S(1)}, u32[]{:S(2)}, u32[]{:S(2)}) collective-permute-start(s32[64,8]{0,1:T(8,128)S(1)} %collective-permute-done.8), channel_id=1, source_target_pairs={{1,0},{2,1},{3,2},{4,3},{5,4},{6,5},{7,6},{8,7},{9,8},{10,9},{11,1... | collective-permute-start | bytes 6152 | tf_op jit(solution)/shard_map/ppermute | solution.py:60
  24.8 4.3 %collective-permute-start.3 = (s32[64,8]{0,1:T(8,128)S(1)}, s32[64,8]{0,1:T(8,128)S(1)}, u32[]{:S(2)}, u32[]{:S(2)}) collective-permute-start(s32[64,8]{0,1:T(8,128)S(1)} %collective-permute-done.2), channel_id=1, source_target_pairs={{0,1},{1,2},{2,3},{3,4},{4,5},{5,6},{6,7},{7,8},{8,9},{9,10},{10,1... | collective-permute-start | bytes 6152 | tf_op jit(solution)/shard_map/ppermute | solution.py:56
  25.7 4.3 %collective-permute-start.10 = (s32[64,8]{0,1:T(8,128)S(1)}, s32[64,8]{0,1:T(8,128)S(1)}, u32[]{:S(2)}, u32[]{:S(2)}) collective-permute-start(s32[64,8]{0,1:T(8,128)S(1)} %collective-permute-done.9), channel_id=1, source_target_pairs={{1,0},{2,1},{3,2},{4,3},{5,4},{6,5},{7,6},{8,7},{9,8},{10,9},{11,1... | collective-permute-start | bytes 6152 | tf_op jit(solution)/shard_map/ppermute | solution.py:60
  29.1 4.7 %collective-permute-start.4 = (s32[64,8]{0,1:T(8,128)S(1)}, s32[64,8]{0,1:T(8,128)S(1)}, u32[]{:S(2)}, u32[]{:S(2)}) collective-permute-start(s32[64,8]{0,1:T(8,128)S(1)} %collective-permute-done.3), channel_id=1, source_target_pairs={{0,1},{1,2},{2,3},{3,4},{4,5},{5,6},{6,7},{7,8},{8,9},{9,10},{10,1... | collective-permute-start | bytes 6152 | tf_op jit(solution)/shard_map/ppermute | solution.py:56
  29.9 4.7 %collective-permute-start.11 = (s32[64,8]{0,1:T(8,128)S(1)}, s32[64,8]{0,1:T(8,128)S(1)}, u32[]{:S(2)}, u32[]{:S(2)}) collective-permute-start(s32[64,8]{0,1:T(8,128)S(1)} %collective-permute-done.10), channel_id=1, source_target_pairs={{1,0},{2,1},{3,2},{4,3},{5,4},{6,5},{7,6},{8,7},{9,8},{10,9},{11,1... | collective-permute-start | bytes 6152 | tf_op jit(solution)/shard_map/ppermute | solution.py:60
  33.8 4.6 %collective-permute-start.5 = (s32[64,8]{0,1:T(8,128)S(1)}, s32[64,8]{0,1:T(8,128)S(1)}, u32[]{:S(2)}, u32[]{:S(2)}) collective-permute-start(s32[64,8]{0,1:T(8,128)S(1)} %collective-permute-done.4), channel_id=1, source_target_pairs={{0,1},{1,2},{2,3},{3,4},{4,5},{5,6},{6,7},{7,8},{8,9},{9,10},{10,1... | collective-permute-start | bytes 6152 | tf_op jit(solution)/shard_map/ppermute | solution.py:56
  34.6 21.7 %collective-permute-start.12 = (s32[64,8]{0,1:T(8,128)S(1)}, s32[64,8]{0,1:T(8,128)S(1)}, u32[]{:S(2)}, u32[]{:S(2)}) collective-permute-start(s32[64,8]{0,1:T(8,128)S(1)} %collective-permute-done.11), channel_id=1, source_target_pairs={{1,0},{2,1},{3,2},{4,3},{5,4},{6,5},{7,6},{8,7},{9,8},{10,9},{11,1... | collective-permute-start | bytes 6152 | tf_op jit(solution)/shard_map/ppermute | solution.py:60
  38.4 18.3 %collective-permute-start.6 = (s32[64,8]{0,1:T(8,128)S(1)}, s32[64,8]{0,1:T(8,128)S(1)}, u32[]{:S(2)}, u32[]{:S(2)}) collective-permute-start(s32[64,8]{0,1:T(8,128)S(1)} %collective-permute-done.5), channel_id=1, source_target_pairs={{0,1},{1,2},{2,3},{3,4},{4,5},{5,6},{6,7},{7,8},{8,9},{9,10},{10,1... | collective-permute-start | bytes 6152 | tf_op jit(solution)/shard_map/ppermute | solution.py:56
  56.4 17.6 %collective-permute-start.13 = (s32[64,8]{0,1:T(8,128)S(1)}, s32[64,8]{0,1:T(8,128)S(1)}, u32[]{:S(2)}, u32[]{:S(2)}) collective-permute-start(s32[64,8]{0,1:T(8,128)S(1)} %collective-permute-done.12), channel_id=1, source_target_pairs={{1,0},{2,1},{3,2},{4,3},{5,4},{6,5},{7,6},{8,7},{9,8},{10,9},{11,1... | collective-permute-start | bytes 6152 | tf_op jit(solution)/shard_map/ppermute | solution.py:60
  56.7 17.4 %collective-permute-start.7 = (s32[64,8]{0,1:T(8,128)S(1)}, s32[64,8]{0,1:T(8,128)S(1)}, u32[]{:S(2)}, u32[]{:S(2)}) collective-permute-start(s32[64,8]{0,1:T(8,128)S(1)} %collective-permute-done.6), channel_id=1, source_target_pairs={{0,1},{1,2},{2,3},{3,4},{4,5},{5,6},{6,7},{7,8},{8,9},{9,10},{10,1... | collective-permute-start | bytes 6152 | tf_op jit(solution)/shard_map/ppermute | solution.py:56
  73.9 3.0 %collective-permute-start.14 = (s32[64,8]{0,1:T(8,128)S(1)}, s32[64,8]{0,1:T(8,128)S(1)}, u32[]{:S(2)}, u32[]{:S(2)}) collective-permute-start(s32[64,8]{0,1:T(8,128)S(1)} %collective-permute-done.13), channel_id=1, source_target_pairs={{1,0},{2,1},{3,2},{4,3},{5,4},{6,5},{7,6},{8,7},{9,8},{10,9},{11,1... | collective-permute-start | bytes 6152 | tf_op jit(solution)/shard_map/ppermute | solution.py:60
  80.5 3.5 %copy-start.2 = (bf16[2,2048,512]{2,1,0:T(8,128)(2,1)S(1)}, bf16[2,2048,512]{2,1,0:T(8,128)(2,1)}, u32[]{:S(2)}) copy-start(bf16[2,2048,512]{2,1,0:T(8,128)(2,1)} %param.14) | copy-start | bytes 12582916
  203.7 5.7 %copy-start.1 = (bf16[64,2048]{1,0:T(8,128)(2,1)}, bf16[64,2048]{1,0:T(8,128)(2,1)S(1)}, u32[]{:S(2)}) copy-start(bf16[64,2048]{1,0:T(8,128)(2,1)S(1)} %reduce_sum.51) | copy-start | bytes 786436
  204.8 4.0 %collective-permute-start.15 = (f32[4]{0:T(128)S(1)}, f32[4]{0:T(128)S(1)}, u32[]{:S(2)}, u32[]{:S(2)}) collective-permute-start(f32[4]{0:T(128)S(1)} %reduce_sum.52), channel_id=1, source_target_pairs={{0,128},{128,0},{16,144},{144,16},{32,160},{160,32},{48,176},{176,... | collective-permute-start | bytes 56 | tf_op jit(solution)/shard_map/ppermute | solution.py:23
Sparse Core Ops, SparseCore 0:
  10.8 46.1 all-gather.3
